TPU v7x, 512 devices: a whole 4x4x16 slice. The times are simulated.
512 devices in a mesh: grp: 16 (over x, y), mlp: 32 (over z, core).
Axes of the slice: x: 4, y: 4, z: 16, core: 2. Of those that a mesh axis runs over, the one named last changes fastest.
Arguments:
- queries: bfloat16 [65536, 4096], P(('grp', 'mlp')), may hold values from -8 to 8
- keys: bfloat16 [65536, 4096], P(('grp', 'mlp')), may hold values from -8 to 8
- values: bfloat16 [65536, 4096], P(('grp', 'mlp')), may hold values from -6 to 6
- gamma: bfloat16 [4096], P('mlp'), may hold values from 0.25 to 2
- w_merge: bfloat16 [4096, 4096], P('grp', 'mlp'), may hold values from -0.09375 to 0.09375
- grids: int32 [256, 2], P('grp'), may hold values from 8 to 16, as said below
- positions: int32 [16384], replicated, may hold values from 0 to 16383, as said below
Outputs:
- prompt_embeds: bfloat16 [16384, 4096], P('grp', 'mlp')
Inputs may be any that keep to these rules, and one draw needn't show every extreme that they name: `grids`: every grid side is even and at least 8; each group has an image of 16 x 16, and a group's images fill at most 4096 slots. positions is a permutation. From one group's 1024 slots at most 128 go to one block of 1024 consecutive prompt positions, and exactly 128 go to some block.
All inputs are finite; a program needn't handle non-finite values.
Results may differ from a plain program's by a relative error of at most 0.015.
Values may be sent and summed in bfloat16 or wider, within the bound.
No kernel may reach another device: no remote copies, remote signals or barrier semaphores. Data moves between devices by JAX's collectives and lax.ppermute only.
A program may use at most 64 MiB of HBM per device.

v0:
```python
import jax
import jax.numpy as jnp
from jax import lax
from jax.sharding import PartitionSpec as P

HD = 128
GRID = 16


def token_layout(grid, gtok):
    heights = grid[:, 0]
    widths = grid[:, 1]
    areas = heights * widths
    ends = jnp.cumsum(areas)
    starts = ends - areas
    count = grid.shape[0]
    slots = jnp.arange(gtok, dtype=jnp.int32)
    image = jnp.sum((slots[:, None] >= ends[None, :]).astype(jnp.int32), axis=1)
    starts_ext = jnp.concatenate([starts, ends[-1:]])
    widths_ext = jnp.concatenate([widths, jnp.full((1,), 2, jnp.int32)])
    onehot = (image[:, None] == jnp.arange(count + 1, dtype=jnp.int32)[None, :]).astype(jnp.int32)
    first = jnp.sum(onehot * starts_ext[None, :], axis=1)
    width = jnp.sum(onehot * widths_ext[None, :], axis=1)
    local = slots - first
    return (image, local // width, local % width)


def pool_layout(grid, gpool):
    heights = grid[:, 0]
    widths = grid[:, 1]
    areas = heights * widths
    ends = jnp.cumsum(areas)
    starts = ends - areas
    count = grid.shape[0]
    slots = jnp.arange(gpool, dtype=jnp.int32)
    image = jnp.sum((slots[:, None] >= (ends // 4)[None, :]).astype(jnp.int32), axis=1)
    starts_ext = jnp.concatenate([starts, ends[-1:]])
    widths_ext = jnp.concatenate([widths, jnp.full((1,), 2, jnp.int32)])
    onehot = (image[:, None] == jnp.arange(count + 1, dtype=jnp.int32)[None, :]).astype(jnp.int32)
    first = jnp.sum(onehot * starts_ext[None, :], axis=1)
    width = jnp.sum(onehot * widths_ext[None, :], axis=1)
    local = slots - first // 4
    half = width // 2
    anchor = first + 2 * (local // half) * width + 2 * (local % half)
    sources = jnp.stack([anchor, anchor + 1, anchor + width, anchor + width + 1], axis=1)
    sources = jnp.clip(sources, 0, 4 * gpool - 1)
    return (sources, image < count)


def rotate(block, row, col):
    quarter = block.shape[2] // 4
    freq = 100.0 ** (-jnp.arange(quarter, dtype=jnp.float32) / quarter)
    ang_row = row.astype(jnp.float32)[:, None, None] * freq[None, None, :]
    ang_col = col.astype(jnp.float32)[:, None, None] * freq[None, None, :]
    full = block.astype(jnp.float32)
    first = full[..., :quarter]
    second = full[..., quarter : 2 * quarter]
    third = full[..., 2 * quarter : 3 * quarter]
    fourth = full[..., 3 * quarter :]
    out = jnp.concatenate(
        [
            first * jnp.cos(ang_row) - second * jnp.sin(ang_row),
            second * jnp.cos(ang_row) + first * jnp.sin(ang_row),
            third * jnp.cos(ang_col) - fourth * jnp.sin(ang_col),
            fourth * jnp.cos(ang_col) + third * jnp.sin(ang_col),
        ],
        axis=-1,
    )
    return out.astype(jnp.bfloat16)


def attend(rot_q, rot_k, vals, image, qrows, margin):
    gtok = rot_q.shape[0]
    scale = rot_q.shape[2] ** (-0.5)
    pad_k = jnp.pad(rot_k, ((margin, margin), (0, 0), (0, 0)))
    pad_v = jnp.pad(vals, ((margin, margin), (0, 0), (0, 0)))
    pad_id = jnp.pad(image, (margin, margin), constant_values=-1)

    def block(index):
        start = index * qrows
        q_blk = lax.dynamic_slice_in_dim(rot_q, start, qrows, 0)
        k_blk = lax.dynamic_slice_in_dim(pad_k, start, qrows + 2 * margin, 0)
        v_blk = lax.dynamic_slice_in_dim(pad_v, start, qrows + 2 * margin, 0)
        q_ids = lax.dynamic_slice_in_dim(image, start, qrows, 0)
        k_ids = lax.dynamic_slice_in_dim(pad_id, start, qrows + 2 * margin, 0)
        scores = (
            jnp.einsum("qhd,khd->hqk", q_blk, k_blk, preferred_element_type=jnp.float32) * scale
        )
        keep = q_ids[:, None] == k_ids[None, :]
        scores = jnp.where(keep[None, :, :], scores, -1e30)
        top = jnp.max(scores, axis=-1, keepdims=True)
        expo = jnp.exp(scores - top)
        probs = (expo / jnp.sum(expo, axis=-1, keepdims=True)).astype(jnp.bfloat16)
        return jnp.einsum("hqk,khd->qhd", probs, v_blk, preferred_element_type=jnp.float32)

    outs = lax.map(block, jnp.arange(gtok // qrows, dtype=jnp.int32))
    return outs.reshape(gtok, rot_q.shape[1], rot_q.shape[2])


def body(queries, keys, values, gamma, w_merge, grids, positions):
    head_q, head_k, head_v = (
        lax.all_to_all(queries, "mlp", split_axis=1, concat_axis=0, tiled=True),
        lax.all_to_all(keys, "mlp", split_axis=1, concat_axis=0, tiled=True),
        lax.all_to_all(values, "mlp", split_axis=1, concat_axis=0, tiled=True),
    )
    gtok = head_q.shape[0]
    width_dev = head_q.shape[1]
    heads_dev = width_dev // HD
    gpool = gtok // 4
    image, row, col = token_layout(grids, gtok)
    rot_q = rotate(head_q.reshape(gtok, heads_dev, HD), row, col)
    rot_k = rotate(head_k.reshape(gtok, heads_dev, HD), row, col)
    attn = attend(
        rot_q, rot_k, head_v.reshape(gtok, heads_dev, HD), image, min(512, gtok), GRID * GRID
    )
    gains = gamma.astype(jnp.float32).reshape(heads_dev, HD)
    branch = (attn * gains[None, :, :]).astype(jnp.bfloat16).reshape(gtok, width_dev)
    sources, valid = pool_layout(grids, gpool)
    picked = jnp.take(branch, sources, axis=0).astype(jnp.float32)
    pooled = jnp.where(valid[:, None], 0.25 * jnp.sum(picked, axis=1), 0.0).astype(jnp.bfloat16)
    full_columns = lax.all_gather(w_merge, "grp", axis=0, tiled=True)
    merged = jnp.dot(
        lax.all_gather(pooled, "mlp", axis=1, tiled=True),
        full_columns,
        preferred_element_type=jnp.float32,
    ).astype(jnp.bfloat16)
    group = lax.axis_index("grp")
    prompt = positions.shape[0]
    source_of = (
        jnp.zeros((prompt,), jnp.int32).at[positions].set(jnp.arange(prompt, dtype=jnp.int32))
    )
    mine = lax.dynamic_slice_in_dim(source_of, group * gpool, gpool, 0)
    everything = lax.all_gather(merged, "grp", axis=0, tiled=True)
    placed = jnp.take(everything, mine, axis=0)
    return placed


def solution(mesh):
    return jax.shard_map(
        body,
        mesh=mesh,
        in_specs=(
            P(("grp", "mlp"), None),
            P(("grp", "mlp"), None),
            P(("grp", "mlp"), None),
            P("mlp"),
            P("grp", "mlp"),
            P("grp", None),
            P(),
        ),
        out_specs=P("grp", "mlp"),
        check_vma=False,
    )
```

profile of v0, /device:TPU:1, one launch (start us, length us, event | category | flops | bytes accessed | tf_op | source)
XLA Modules:
  0.0 445.1 jit_solution(18084548913521165497)
XLA Ops:
  6.5 2.4 copy.48
  8.9 16.7 %all-to-all-start.1 = ((bf16[128,32,128]{0,2,1:T(8,128)(2,1)}), bf16[128,32,128]{0,2,1:T(8,128)(2,1)S(1)}, u32[]{:S(2)}, u32[]{:S(2)}) async-start(bf16[128,32,128]{0,2,1:T(8,128)(2,1)} %bitcast.15), calls=%async_computation.1 | async-start | bytes 2097152 | tf_op jit(solution)/shard_map/all_to_all | solution.py:102
  27.0 54.4 %all-to-all-done.1 = bf16[128,32,128]{0,2,1:T(8,128)(2,1)S(1)} async-done(((bf16[128,32,128]{0,2,1:T(8,128)(2,1)}), bf16[128,32,128]{0,2,1:T(8,128)(2,1)S(1)}, u32[]{:S(2)}, u32[]{:S(2)}) %all-to-all-start.1) | async-done | bytes 1048608 | tf_op jit(solution)/shard_map/all_to_all | solution.py:102
  81.4 4.1 all-to-all-start.2
  86.9 54.4 %all-to-all-done.2 = bf16[128,32,128]{0,2,1:T(8,128)(2,1)S(1)} async-done(((bf16[128,32,128]{0,2,1:T(8,128)(2,1)}), bf16[128,32,128]{0,2,1:T(8,128)(2,1)S(1)}, u32[]{:S(2)}, u32[]{:S(2)}) %all-to-all-start.2) | async-done | bytes 1048608 | tf_op jit(solution)/shard_map/all_to_all | solution.py:103
  141.3 5.3 %all-to-all-start = ((bf16[128,32,128]{0,2,1:T(8,128)(2,1)}), bf16[128,32,128]{0,2,1:T(8,128)(2,1)}, u32[]{:S(2)}, u32[]{:S(2)}) async-start(bf16[128,32,128]{0,2,1:T(8,128)(2,1)} %bitcast.12), calls=%async_computation | async-start | bytes 2097152 | tf_op jit(solution)/shard_map/all_to_all | solution.py:104
  151.9 2.5 copy.49
  154.4 1.7 reshape.802
  156.4 2.6 copy.51
  158.9 2.7 reshape.803
  161.6 40.8 %all-to-all-done = bf16[128,32,128]{0,2,1:T(8,128)(2,1)} async-done(((bf16[128,32,128]{0,2,1:T(8,128)(2,1)}), bf16[128,32,128]{0,2,1:T(8,128)(2,1)}, u32[]{:S(2)}, u32[]{:S(2)}) %all-to-all-start) | async-done | bytes 1048608 | tf_op jit(solution)/shard_map/all_to_all | solution.py:104
  206.1 4.5 %fusion.31 = (bf16[4096,1,32]{0,2,1:T(8,128)(2,1)S(1)}, bf16[4096,1,32]{0,2,1:T(8,128)(2,1)S(1)}, bf16[4096,1,32]{0,2,1:T(8,128)(2,1)S(1)}, bf16[4096,1,32]{0,2,...) fusion(f32[4096,1,128]{0,2,1:T(8,128)S(1)} %reshape.802, ...), kind=kLoop, calls=%fused_computation.53 | loop fusion | flops 4456448 | bytes 6324352 | tf_op jit(solution)/shard_map/convert.8
  212.8 42.0 %while.10 = (s32[]{:T(128)}, f32[8,512,1,128]{3,1,0,2:T(8,128)S(1)}, s32[8]{0:T(128)S(1)}, bf16[4608,1,128]{2,0,1:T(8,128)(2,1)}, s32[4096]{0:T(1024)S(1)}, /*in...) while((s32[]{:T(128)}, ...), condition=%wide.region_11.12_spmd, body=%wide.region_8.11_spmd.sunk | while | flops 273153024 | bytes 8286440 | solution.py:96
  216.2 1.6 convolution_bitcast_fusion.2
  232.0 1.6 convolution_bitcast_fusion.2
  237.3 1.6 convolution_bitcast_fusion.2
  253.0 1.6 convolution_bitcast_fusion.2
  255.0 12.1 %gather_fusion = bf16[4096,128]{1,0:T(8,128)(2,1)S(1)} fusion(bf16[4096,128]{1,0:T(8,128)(2,1)S(1)} %fusion.10, s32[4096]{0:T(1024)S(1)} %broadcast_clamp_fusion), kind=kCustom, calls=%fused_computation | custom fusion | bytes 2113536 | tf_op jit(solution)/shard_map/jit(_take)/gather | solution.py:119
  267.1 5.8 %convert_reduce_fusion = f32[1024,128]{1,0:T(8,128)S(1)} fusion(bf16[1024,4,128]{2,1,0:T(4,128)(2,1)S(1)} %bitcast.71, pred[1024,4]{1,0:T(8,128)(4,1)S(1)} %copy.45), kind=kLoop, calls=%fused_computation.24 | loop fusion | flops 1441792 | bytes 1576960 | tf_op jit(solution)/shard_map/reduce_sum | solution.py:120
  274.2 88.9 %all-gather.4.cloned.1.call-done = bf16[1024,4096]{1,0:T(8,128)(2,1)} async-done(((bf16[1024,128]{1,0:T(8,128)(2,1)}), bf16[1024,4096]{1,0:T(8,128)(2,1)}) %all-gather.4.cloned.1.call-update) | async-done | bytes 8388624 | tf_op jit(solution)/shard_map/all_gather | solution.py:123
  363.1 6.6 %convolution_convert_fusion = bf16[1024,128]{1,0:T(8,128)(2,1)} fusion(bf16[1024,4096]{1,0:T(8,128)(2,1)} %all-gather.4.cloned.1.call-done, bf16[4096,128]{1,0:T(8,128)(2,1)} %all-gather.6.cloned.1.call-done), kind=kOutput, calls=%fused_computation.25 | convolution fusion | flops 1073872896 | bytes 9699328 | tf_op jit(solution)/shard_map/dot_general | solution.py:122
  369.8 60.3 %scatter_custom_fusion = s32[16384]{0:T(1024)S(1)} fusion(s32[16384]{0:T(1024)S(1)} %compare_select_fusion, s32[16384]{0:T(1024)S(1)} %iota.40, s32[]{:T(128)} %constant.124.clone.1), kind=kCustom, calls=%fused_computation.84 | custom fusion | bytes 65540 | tf_op jit(solution)/shard_map/scatter | solution.py:130
  430.2 1.8 all-gather.8.cloned.1.call-done
  432.0 5.6 %gather_fusion.1 = bf16[1024,128]{1,0:T(8,128)(2,1)S(1)} fusion(bf16[16384,128]{1,0:T(8,128)(2,1)} %all-gather.8.cloned.1.call-done, s32[1024]{0:T(1024)S(1)} %fusion.52), kind=kCustom, calls=%fused_computation.1 | custom fusion | bytes 528384 | tf_op jit(solution)/shard_map/jit(_take)/gather | solution.py:134
  (123 shorter events, 46.8 us)
Async XLA Ops:
  6.5 19.1 %copy-start.2 = (bf16[128,4096]{1,0:T(8,128)(2,1)S(1)}, bf16[128,4096]{1,0:T(8,128)(2,1)}, u32[]{:S(2)}) copy-start(bf16[128,4096]{1,0:T(8,128)(2,1)} %param.10) | copy-start | bytes 3145732
  8.9 72.5 %all-to-all-start.1 = ((bf16[128,32,128]{0,2,1:T(8,128)(2,1)}), bf16[128,32,128]{0,2,1:T(8,128)(2,1)S(1)}, u32[]{:S(2)}, u32[]{:S(2)}) async-start(bf16[128,32,128]{0,2,1:T(8,128)(2,1)} %bitcast.15), calls=%async_computation.1 | async-start | bytes 2097152 | tf_op jit(solution)/shard_map/all_to_all | solution.py:102
  27.0 58.5 %copy-start.3 = (bf16[128,4096]{1,0:T(8,128)(2,1)S(1)}, bf16[128,4096]{1,0:T(8,128)(2,1)}, u32[]{:S(2)}) copy-start(bf16[128,4096]{1,0:T(8,128)(2,1)} %param.11) | copy-start | bytes 3145732
  81.4 59.9 %all-to-all-start.2 = ((bf16[128,32,128]{0,2,1:T(8,128)(2,1)}), bf16[128,32,128]{0,2,1:T(8,128)(2,1)S(1)}, u32[]{:S(2)}, u32[]{:S(2)}) async-start(bf16[128,32,128]{0,2,1:T(8,128)(2,1)} %bitcast.17), calls=%async_computation.2 | async-start | bytes 2097152 | tf_op jit(solution)/shard_map/all_to_all | solution.py:103
  85.5 62.1 %copy-start.5 = (s32[16,2]{0,1:T(2,128)S(1)}, s32[16,2]{0,1:T(2,128)}, u32[]{:S(2)}) copy-start(s32[16,2]{0,1:T(2,128)} %param.14) | copy-start | bytes 388
  85.5 62.8 %copy-start.6 = (bf16[128]{0:T(256)(128)(2,1)S(1)}, bf16[128]{0:T(256)(128)(2,1)}, u32[]{:S(2)}) copy-start(bf16[128]{0:T(256)(128)(2,1)} %param.12) | copy-start | bytes 772
  141.3 61.2 %all-to-all-start = ((bf16[128,32,128]{0,2,1:T(8,128)(2,1)}), bf16[128,32,128]{0,2,1:T(8,128)(2,1)}, u32[]{:S(2)}, u32[]{:S(2)}) async-start(bf16[128,32,128]{0,2,1:T(8,128)(2,1)} %bitcast.12), calls=%async_computation | async-start | bytes 2097152 | tf_op jit(solution)/shard_map/all_to_all | solution.py:104
  146.6 127.6 %all-gather.6.cloned.1.call-start = ((), (), s32[]{:S(2)}) async-start(), calls=%async_computation.4 | async-start | bytes 1114112 | tf_op jit(solution)/shard_map/all_gather | solution.py:121
  147.3 215.8 %all-gather.4.cloned.1.call-start = ((), (), s32[]{:S(2)}) async-start(), calls=%async_computation.3 | async-start | bytes 8650752 | tf_op jit(solution)/shard_map/all_gather | solution.py:123
  204.1 2.0 copy-start
  210.6 2.2 copy-start.1
  273.9 95.9 %copy-start.4 = (s32[16384]{0:T(1024)S(1)}, s32[16384]{0:T(1024)}, u32[]{:S(2)}) copy-start(s32[16384]{0:T(1024)} %param.15) | copy-start | bytes 196612
  273.9 158.1 %all-gather.8.cloned.1.call-start = ((), (), s32[]{:S(2)}) async-start(), calls=%async_computation.5 | async-start | bytes 4456448 | tf_op jit(solution)/shard_map/all_gather | solution.py:133
Sparse Core Ops, SparseCore 0:
  150.4 57.3 all-gather.5
  274.0 89.0 all-gather.3
  369.9 62.0 all-gather.7
where the time goes:
time: 446 us; the launch traced here: 445 us
  waiting for transfers between devices  241 us (54%)
  local copies, waits for them, and re-layouts  105 us (24%)
  matrix products  32.6 us (7%)
  starting transfers between devices  26.6 us (6%)
  other arithmetic  21.6 us (5%)
  between operations  13.4 us (3%)
  loops' own time  4.91 us (1%)
    all_gather x1, waiting for transfers between devices, body(): lax.all_gather(pooled, 'mlp', axis=1, tiled=True)  88.9 us
    scatter x1, local copies, waits for them, and re-layouts, body(): jnp.zeros((prompt,), jnp.int32).at[positions]  60.3 us
    all_to_all x1, waiting for transfers between devices, body(): lax.all_to_all(keys, 'mlp', split_axis=1, concat_axis=0, tiled=True)  54.4 us
    all_to_all x1, waiting for transfers between devices, body(): lax.all_to_all(queries, 'mlp', split_axis=1, concat_axis=0, tiled=True)  54.4 us
    all_to_all x1, waiting for transfers between devices, body(): lax.all_to_all(values, 'mlp', split_axis=1, concat_axis=0, tiled=True)  40.8 us
    all_to_all x1, starting transfers between devices, body(): lax.all_to_all(queries, 'mlp', split_axis=1, concat_axis=0, tiled=True)  16.7 us
    dot_general x8, matrix products, block(): jnp.einsum('hqk,khd->qhd', probs, v_blk, preferred_element_type=jnp.float32)  13.1 us
    dot_general x8, matrix products, block(): jnp.einsum('qhd,khd->hqk', q_blk, k_blk, preferred_element_type=jnp.float32)  12.8 us
  transfers between devices with their start and end apart: 6, of which 5 were waited for; matrix products, arithmetic and copies ran while one was open for 32% of the time, Pallas kernels for 0%

commit v1 on v0

--- a/solution.py
+++ b/solution.py
@@ -119,11 +119,16 @@
     picked = jnp.take(branch, sources, axis=0).astype(jnp.float32)
     pooled = jnp.where(valid[:, None], 0.25 * jnp.sum(picked, axis=1), 0.0).astype(jnp.bfloat16)
     full_columns = lax.all_gather(w_merge, "grp", axis=0, tiled=True)
-    merged = jnp.dot(
-        lax.all_gather(pooled, "mlp", axis=1, tiled=True),
-        full_columns,
-        preferred_element_type=jnp.float32,
-    ).astype(jnp.bfloat16)
+
+    def _start_tasks(slab_in, mesh_dim="mlp"):
+        n_now = lax.all_to_all(
+            jnp.stack([slab_in for _ in range(lax.axis_size(mesh_dim))]), mesh_dim, 0, 0
+        )
+        return jnp.concatenate(n_now, axis=1)
+
+    merged = jnp.dot(_start_tasks(pooled), full_columns, preferred_element_type=jnp.float32).astype(
+        jnp.bfloat16
+    )
     group = lax.axis_index("grp")
     prompt = positions.shape[0]
     source_of = (

time: 446 us -> 734 us (1.65)
  waiting for transfers between devices: 241 us -> 519 us
    all_to_all x0 -> x1, waiting for transfers between devices: none -> 299 us  [_start_tasks(): lax.all_to_all(jnp.stack([slab_in for _ in range(lax.axis_size(mesh_dim))...]
    all_gather x1 -> x0, waiting for transfers between devices: 88.9 us -> none  [body(): lax.all_gather(pooled, 'mlp', axis=1, tiled=True)]
    all_gather x1, waiting for transfers between devices: 0.02 us -> 60.6 us  [body(): full_columns = lax.all_gather(w_merge, 'grp', axis=0, tiled=True)]
  transfers between devices with their start and end apart: 6 -> 6, of which waited for: 5 -> 6; matrix products, arithmetic and copies ran while one was open for 32% -> 11% of each run, Pallas kernels for 0% -> 0%
where the time goes in v1:
time: 734 us; the launch traced here: 732 us
  waiting for transfers between devices  519 us (71%)
  local copies, waits for them, and re-layouts  109 us (15%)
  matrix products  32.6 us (4%)
  starting transfers between devices  32 us (4%)
  other arithmetic  20.9 us (3%)
  between operations  13.7 us (2%)
    all_to_all x1, waiting for transfers between devices, _start_tasks(): lax.all_to_all(jnp.stack([slab_in for _ in range(lax.axis_size(mesh_dim))...  299 us
    all_gather x1, waiting for transfers between devices, body(): full_columns = lax.all_gather(w_merge, 'grp', axis=0, tiled=True)  60.6 us
    scatter x1, local copies, waits for them, and re-layouts, body(): jnp.zeros((prompt,), jnp.int32).at[positions]  60.3 us
    all_to_all x1, waiting for transfers between devices, body(): lax.all_to_all(keys, 'mlp', split_axis=1, concat_axis=0, tiled=True)  54.4 us
    all_to_all x1, waiting for transfers between devices, body(): lax.all_to_all(queries, 'mlp', split_axis=1, concat_axis=0, tiled=True)  54.4 us
    all_to_all x1, waiting for transfers between devices, body(): lax.all_to_all(values, 'mlp', split_axis=1, concat_axis=0, tiled=True)  41.7 us
    all_to_all x1, starting transfers between devices, body(): lax.all_to_all(queries, 'mlp', split_axis=1, concat_axis=0, tiled=True)  16.7 us
  transfers between devices with their start and end apart: 6, of which 6 were waited for; matrix products, arithmetic and copies ran while one was open for 11% of the time, Pallas kernels for 0%

profile of v1, /device:TPU:1, one launch (start us, length us, event | category | flops | bytes accessed | tf_op | source)
XLA Modules:
  0.0 732.3 jit_solution(5439666161532797573)
XLA Ops:
  6.5 2.4 copy.59
  8.9 16.7 %all-to-all-start.1 = ((bf16[128,32,128]{0,2,1:T(8,128)(2,1)}), bf16[128,32,128]{0,2,1:T(8,128)(2,1)S(1)}, u32[]{:S(2)}, u32[]{:S(2)}) async-start(bf16[128,32,128]{0,2,1:T(8,128)(2,1)} %bitcast.15), calls=%async_computation.1 | async-start | bytes 2097152 | tf_op jit(solution)/shard_map/all_to_all | solution.py:102
  27.0 54.4 %all-to-all-done.1 = bf16[128,32,128]{0,2,1:T(8,128)(2,1)S(1)} async-done(((bf16[128,32,128]{0,2,1:T(8,128)(2,1)}), bf16[128,32,128]{0,2,1:T(8,128)(2,1)S(1)}, u32[]{:S(2)}, u32[]{:S(2)}) %all-to-all-start.1) | async-done | bytes 1048608 | tf_op jit(solution)/shard_map/all_to_all | solution.py:102
  81.4 4.1 all-to-all-start.2
  86.9 54.4 %all-to-all-done.2 = bf16[128,32,128]{0,2,1:T(8,128)(2,1)S(1)} async-done(((bf16[128,32,128]{0,2,1:T(8,128)(2,1)}), bf16[128,32,128]{0,2,1:T(8,128)(2,1)S(1)}, u32[]{:S(2)}, u32[]{:S(2)}) %all-to-all-start.2) | async-done | bytes 1048608 | tf_op jit(solution)/shard_map/all_to_all | solution.py:103
  141.3 5.3 all-to-all-start
  150.9 2.5 copy.60
  153.4 1.7 reshape.818
  155.4 2.6 copy.62
  158.0 2.7 reshape.819
  160.7 41.7 %all-to-all-done = bf16[128,32,128]{0,2,1:T(8,128)(2,1)} async-done(((bf16[128,32,128]{0,2,1:T(8,128)(2,1)}), bf16[128,32,128]{0,2,1:T(8,128)(2,1)}, u32[]{:S(2)}, u32[]{:S(2)}) %all-to-all-start) | async-done | bytes 1048608 | tf_op jit(solution)/shard_map/all_to_all | solution.py:104
  206.1 4.5 fusion.31
  212.8 42.0 %while.10 = (s32[]{:T(128)}, f32[8,512,1,128]{3,1,0,2:T(8,128)S(1)}, s32[8]{0:T(128)S(1)}, bf16[4608,1,128]{2,0,1:T(8,128)(2,1)}, s32[4096]{0:T(1024)S(1)}, /*in...) while((s32[]{:T(128)}, ...), condition=%wide.region_11.12_spmd, body=%wide.region_8.11_spmd.sunk | while | flops 273153024 | bytes 8286440 | solution.py:96
  216.2 1.6 convolution_bitcast_fusion.2
  254.9 12.1 %gather_fusion = bf16[4096,128]{1,0:T(8,128)(2,1)S(1)} fusion(bf16[4096,128]{1,0:T(8,128)(2,1)S(1)} %fusion.10, s32[4096]{0:T(1024)S(1)} %broadcast_clamp_fusion), kind=kCustom, calls=%fused_computation | custom fusion | bytes 2113536 | tf_op jit(solution)/shard_map/jit(_take)/gather | solution.py:119
  267.1 5.8 convert_reduce_fusion
  273.3 4.3 stack.20
  277.6 5.6 all-to-all-start.3
  284.1 60.6 %all-gather.3.cloned.1.call-done = bf16[4096,128]{1,0:T(8,128)(2,1)} async-done(((bf16[256,128]{1,0:T(8,128)(2,1)}), bf16[4096,128]{1,0:T(8,128)(2,1)}) %all-gather.3.cloned.1.call-update) | async-done | bytes 1048592 | tf_op jit(solution)/shard_map/all_gather | solution.py:121
  344.7 298.9 %all-to-all-done.3 = bf16[32,1024,128]{1,2,0:T(8,128)(2,1)} async-done(((bf16[32,1024,128]{1,2,0:T(8,128)(2,1)}), bf16[32,1024,128]{1,2,0:T(8,128)(2,1)}, u32[]{:S(2)}, u32[]{:S(2)}) %all-to-all-start.3) | async-done | bytes 8388640 | tf_op jit(solution)/shard_map/all_to_all | solution.py:124
  643.7 6.7 convolution_convert_fusion
  650.5 60.3 %scatter_custom_fusion = s32[16384]{0:T(1024)S(1)} fusion(s32[16384]{0:T(1024)S(1)} %compare_select_fusion, s32[16384]{0:T(1024)S(1)} %iota.40, s32[]{:T(128)} %constant.124.clone.1), kind=kCustom, calls=%fused_computation.84 | custom fusion | bytes 65540 | tf_op jit(solution)/shard_map/scatter | solution.py:135
  710.9 8.1 %all-gather.5.cloned.1.call-done = bf16[16384,128]{1,0:T(8,128)(2,1)} async-done(((bf16[1024,128]{1,0:T(8,128)(2,1)}), bf16[16384,128]{1,0:T(8,128)(2,1)}) %all-gather.5.cloned.1.call-update) | async-done | bytes 4194320 | tf_op jit(solution)/shard_map/all_gather | solution.py:138
  719.0 5.6 gather_fusion.1
  (124 shorter events, 50.8 us)
Async XLA Ops:
  6.5 19.1 %copy-start.2 = (bf16[128,4096]{1,0:T(8,128)(2,1)S(1)}, bf16[128,4096]{1,0:T(8,128)(2,1)}, u32[]{:S(2)}) copy-start(bf16[128,4096]{1,0:T(8,128)(2,1)} %param.10) | copy-start | bytes 3145732
  8.9 72.5 %all-to-all-start.1 = ((bf16[128,32,128]{0,2,1:T(8,128)(2,1)}), bf16[128,32,128]{0,2,1:T(8,128)(2,1)S(1)}, u32[]{:S(2)}, u32[]{:S(2)}) async-start(bf16[128,32,128]{0,2,1:T(8,128)(2,1)} %bitcast.15), calls=%async_computation.1 | async-start | bytes 2097152 | tf_op jit(solution)/shard_map/all_to_all | solution.py:102
  27.0 58.5 %copy-start.3 = (bf16[128,4096]{1,0:T(8,128)(2,1)S(1)}, bf16[128,4096]{1,0:T(8,128)(2,1)}, u32[]{:S(2)}) copy-start(bf16[128,4096]{1,0:T(8,128)(2,1)} %param.11) | copy-start | bytes 3145732
  81.4 59.9 %all-to-all-start.2 = ((bf16[128,32,128]{0,2,1:T(8,128)(2,1)}), bf16[128,32,128]{0,2,1:T(8,128)(2,1)S(1)}, u32[]{:S(2)}, u32[]{:S(2)}) async-start(bf16[128,32,128]{0,2,1:T(8,128)(2,1)} %bitcast.17), calls=%async_computation.2 | async-start | bytes 2097152 | tf_op jit(solution)/shard_map/all_to_all | solution.py:103
  85.5 61.1 %copy-start.5 = (s32[16,2]{0,1:T(2,128)S(1)}, s32[16,2]{0,1:T(2,128)}, u32[]{:S(2)}) copy-start(s32[16,2]{0,1:T(2,128)} %param.14) | copy-start | bytes 388
  85.5 61.9 %copy-start.6 = (bf16[128]{0:T(256)(128)(2,1)S(1)}, bf16[128]{0:T(256)(128)(2,1)}, u32[]{:S(2)}) copy-start(bf16[128]{0:T(256)(128)(2,1)} %param.12) | copy-start | bytes 772
  141.3 61.2 %all-to-all-start = ((bf16[128,32,128]{0,2,1:T(8,128)(2,1)}), bf16[128,32,128]{0,2,1:T(8,128)(2,1)}, u32[]{:S(2)}, u32[]{:S(2)}) async-start(bf16[128,32,128]{0,2,1:T(8,128)(2,1)} %bitcast.12), calls=%async_computation | async-start | bytes 2097152 | tf_op jit(solution)/shard_map/all_to_all | solution.py:104
  204.1 2.0 copy-start
  210.6 2.2 copy-start.1
  277.6 366.1 %all-to-all-start.3 = ((bf16[32,1024,128]{1,2,0:T(8,128)(2,1)}), bf16[32,1024,128]{1,2,0:T(8,128)(2,1)}, u32[]{:S(2)}, u32[]{:S(2)}) async-start(bf16[32,1024,128]{1,2,0:T(8,128)(2,1)} %stack.20), calls=%async_computation.3 | async-start | bytes 16777216 | tf_op jit(solution)/shard_map/all_to_all | solution.py:124
  283.1 61.6 %all-gather.3.cloned.1.call-start = ((), (), s32[]{:S(2)}) async-start(), calls=%async_computation.4 | async-start | bytes 1114112 | tf_op jit(solution)/shard_map/all_gather | solution.py:121
  283.9 435.1 %all-gather.5.cloned.1.call-start = ((), (), s32[]{:S(2)}) async-start(), calls=%async_computation.5 | async-start | bytes 4456448 | tf_op jit(solution)/shard_map/all_gather | solution.py:138
  643.7 6.8 copy-start.4
Sparse Core Ops, SparseCore 0:
  287.0 57.6 all-gather.2
  650.6 68.3 all-gather.4
